TPU v7x, 128 devices: a whole 4x4x4 slice. The times are simulated.
128 devices in a mesh: lat: 8 (over x, core), lon: 16 (over y, z).
Axes of the slice: x: 4, y: 4, z: 4, core: 2. Of those that a mesh axis runs over, the one named last changes fastest.
Arguments:
- prior: float32 [1024, 32768], P('lat', 'lon'), may hold values from 0.005 to 120
- zone_ids: int32 [1024, 32768], P('lat', 'lon'), may hold values from 0 to 4095, as said below
- rate: float32 [4096], replicated, may hold values from 0.3 to 3
Outputs:
- density: float32 [1024, 32768], P('lat', 'lon')
Inputs may be any that keep to these rules, and one draw needn't show every extreme that they name: `zone_ids`: provinces are unions of aligned blocks of 8 rows by 64 columns, except that in the last 16 columns of a block some cells take the province of the block to the east (longitude wrapping); every province owns at least one whole block.
All inputs are finite; a program needn't handle non-finite values.
Results may differ from a plain program's by a relative error of at most 0.0002.
Values sent between devices are 32-bit elements; how exact they have to be, the bound alone decides.
A program may use at most 64 MiB of HBM per device.

v0:
```python
import jax
import jax.numpy as jnp
from jax import lax
from jax.experimental import pallas as pl
from jax.experimental.pallas import tpu as pltpu
from jax.sharding import PartitionSpec as P

ROWS, COLS = 128, 2048
STEP = 16
TILES = COLS // 128
SWEEPS = 3
DEPTH = 6
IDS = 3
SIDE = STEP + DEPTH
GROUPS = 10
MESH = pl.DeviceIdType.MESH
F32, I32, BF16 = jnp.float32, jnp.int32, jnp.bfloat16


def split2(x):
    high = x.astype(BF16)
    low = (x - high.astype(F32)).astype(BF16)
    return jnp.concatenate([high, low], axis=0)


def place(row, col):
    return {"lat": lax.rem(row + 8, 8), "lon": lax.rem(col + 16, 16)}


def device(x, core, y, z):
    return (lax.rem(x, 4) * 2 + core, lax.rem(y, 4) * 4 + lax.rem(z, 4))


FAR_A = [2, 3, 1, 0]
FAR_B = sorted(
    [(a, b) for a in range(4) for b in range(4) if (a, b) != (0, 0)],
    key=lambda t: -(min(t[0], 4 - t[0]) + min(t[1], 4 - t[1])),
)


def drain(ref, sem):
    pltpu.make_async_copy(ref, ref, sem).wait()


def kernel(
    prior, zones, rate, out,
    pin, zin, turn, iturn, level, ids,
    prow, pcol, pcorner, zrow, zcol, zcorner, ppack, zpack,
    onehot_hi, onehot_lo,
    part, part_in, half, half_in, factors,
    load_sem, store_sem, rate_sem, halo_send, halo_recv, zhalo_send, zhalo_recv,
    a_send, a_recv, b_send, b_recv, c_send, c_recv, rate_in,
):
    lat, lon = lax.axis_index("lat"), lax.axis_index("lon")
    x, core = lax.div(lat, 2), lax.rem(lat, 2)
    y, z = lax.div(lon, 4), lax.rem(lon, 4)

    around = [(-1, 0), (1, 0), (0, -1), (0, 1), (-1, -1), (-1, 1), (1, -1), (1, 1)]
    a_peers = []
    for d in FAR_A:
        for flip in (1, 0):
            if (d, flip) != (0, 0):
                a_peers.append((d * 2 + flip, flip, device(x + d, jnp.where(flip == 1, 1 - core, core), y, z)))
    b_peers = [(i, device(x, core, y + a, z + b)) for i, (a, b) in enumerate(FAR_B)]
    partner = device(x, 1 - core, y, z)

    barrier = pltpu.get_barrier_semaphore()
    greeted = 0
    for dr, dc in around:
        pl.semaphore_signal(barrier, inc=1, device_id=place(lat + dr, lon + dc), device_id_type=MESH)
        greeted += 1

    def tile(t):
        return slice(128 * t, 128 * t + 128)

    for n, t in [(0, 0), (0, TILES - 1), (1, 0), (1, TILES - 1)] + [(n, t) for n in (0, 1) for t in range(1, TILES - 1)]:
        sem = load_sem.at[n, 0 if t == 0 else 1 if t == TILES - 1 else 2]
        pltpu.make_async_copy((prior, zones)[n].at[:, tile(t)], (pin, zin)[n].at[t], sem).start()
    rate_copy = pltpu.make_async_copy(rate, rate_in, rate_sem)
    rate_copy.start()

    for _, _, peer in a_peers:
        pl.semaphore_signal(barrier, inc=1, device_id=peer, device_id_type=MESH)
        greeted += 1
    for _, peer in b_peers:
        pl.semaphore_signal(barrier, inc=1, device_id=peer, device_id_type=MESH)
        greeted += 1

    lane = lax.broadcasted_iota(I32, (8, 128), 1)
    q = lax.broadcasted_iota(I32, (8, 128), 0)
    s = lax.rem(lane, 8)
    mirror_top = s + 8 * lat < 4
    mirror_bottom = s + 8 * lat >= 60

    def pick(value, index):
        return jnp.take_along_axis(value, index, axis=1, mode="promise_in_bounds")

    def spread(row, shape=(8, 128)):
        return jnp.broadcast_to(row, shape)

    def pack(ref, packed):
        index = 16 * s + lax.div(lane, 8)
        packed[0] = pick(ref[0].T[0:8], index)
        packed[1] = pick(ref[TILES - 1].T[120:128], index)

    first8, last8 = pl.ds(0, 8), pl.ds(ROWS - 8, 8)
    first128, last128 = pl.ds(0, 128), pl.ds(COLS - 128, 128)

    def send(src, dst, send_sem, recv_sem, dr, dc):
        pltpu.make_async_remote_copy(
            src_ref=src, dst_ref=dst, send_sem=send_sem, recv_sem=recv_sem,
            device_id=place(lat + dr, lon + dc), device_id_type=MESH,
        ).start()

    def send_rows(source, row_in, corner_in, out_sem, in_sem):
        send(source.at[first8, first128], corner_in.at[2], out_sem.at[2], in_sem.at[2], -1, -1)
        send(source.at[first8, last128], corner_in.at[3], out_sem.at[2], in_sem.at[2], -1, 1)
        send(source.at[last8, first128], corner_in.at[0], out_sem.at[2], in_sem.at[2], 1, -1)
        send(source.at[last8, last128], corner_in.at[1], out_sem.at[2], in_sem.at[2], 1, 1)
        send(source.at[first8, :], row_in.at[1], out_sem.at[0], in_sem.at[0], -1, 0)
        send(source.at[last8, :], row_in.at[0], out_sem.at[0], in_sem.at[0], 1, 0)

    def send_cols(packed, col_in, out_sem, in_sem):
        send(packed.at[0], col_in.at[0], out_sem.at[1], in_sem.at[1], 0, -1)
        send(packed.at[1], col_in.at[1], out_sem.at[1], in_sem.at[1], 0, 1)

    drain(pin.at[0], load_sem.at[0, 0])
    drain(pin.at[TILES - 1], load_sem.at[0, 1])
    pack(pin, ppack)
    pl.semaphore_wait(barrier, greeted)
    send_cols(ppack, pcol, halo_send, halo_recv)
    send_rows(prior, prow, pcorner, halo_send, halo_recv)
    drain(zin.at[0], load_sem.at[1, 0])
    drain(zin.at[TILES - 1], load_sem.at[1, 1])
    pack(zin, zpack)
    send_cols(zpack, zcol, zhalo_send, zhalo_recv)
    send_rows(zones, zrow, zcorner, zhalo_send, zhalo_recv)

    inner = pl.ds(1, TILES - 2)

    def turned(matrix, slot):
        buffer = turn if matrix.dtype == F32 else iturn
        buffer[slot] = matrix.T
        return [buffer.at[slot][pl.ds(t, 8, stride=STEP), :] for t in range(STEP)]

    def load_planes(ref, write):
        for r in range(STEP):
            rows = [ref.at[t][pl.ds(r, 8, stride=STEP), :] for t in range(TILES)]
            for t, value in enumerate(turned(jnp.concatenate(rows, axis=0), r % 4)):
                write(r, t, value)

    def write_prior(r, t, value):
        level[0, r, t] = value

    def write_ids(r, t, value):
        ids[r, t] = value

    drain(pin.at[inner], load_sem.at[0, 2])
    load_planes(pin, write_prior)
    drain(zin.at[inner], load_sem.at[1, 2])
    load_planes(zin, write_ids)

    hi_iota = lax.broadcasted_iota(I32, (32, 128), 0)
    lo_iota = lax.broadcasted_iota(I32, (128, 128), 0)

    def encode(line, group):
        hi = jnp.right_shift(line, 7)
        lo = jnp.bitwise_and(line, 127)
        onehot_hi[group] = jnp.where(hi_iota == hi, 1.0, 0.0)
        onehot_lo[:, 128 * group : 128 * group + 128] = jnp.where(lo_iota == lo, 1.0, 0.0).astype(BF16)

    def own_ids(row):
        value = ids[row, 0]
        return [value[0:1], value[4:5]], jnp.where(q < 4, spread(value[0:1]), spread(value[4:5]))

    own = []
    for h in range(2):
        lines, cells = own_ids(8 * h)
        own.append(cells)
        for g in range(2):
            encode(lines[g], 2 * h + g)

    def fold(value):
        value = value + pltpu.roll(value, 7, 0)
        value = value + pltpu.roll(value, 6, 0)
        return value[0:1], value[4:5]

    def scatter(pairs):
        lines, ext = [], []
        for own_sum, east_sum in pairs:
            own0, own1 = fold(own_sum)
            east0, east1 = fold(east_sum)
            east1 = spread(east1)
            beyond = pltpu.roll(east1, 8, 1)[0:1]
            lines.append(own0 + jnp.where(lane[0:1] >= 8, beyond, 0.0))
            lines.append(own1 + east0)
            ext.append((east1[0:1], beyond))
        lines.append(jnp.where(lane[0:1] >= 120, ext[0][0], jnp.where(lane[0:1] < 8, ext[1][1], 0.0)))
        weighted = split2(jnp.concatenate([onehot_hi[g] * lines[g] for g in range(5)], axis=1))
        table = lax.dot_general(
            weighted, onehot_lo[:, 0:640], (((1,), (1,)), ((), ())), preferred_element_type=F32
        )
        return table[0:32] + table[32:64]

    def block_sums(n, h):
        own_sum, east_sum = jnp.zeros((STEP, 8, 128), F32), jnp.zeros((STEP, 8, 128), F32)
        for r in range(8 * h, 8 * h + 8):
            matched = ids[r, 0:STEP] == own[h]
            value = level[n, r, 0:STEP]
            own_sum += jnp.where(matched, value, 0.0)
            east_sum += jnp.where(matched, 0.0, value)
        return jnp.sum(own_sum, axis=0), jnp.sum(east_sum, axis=0)

    counts, others = [], []
    for h in range(2):
        own_sum = jnp.zeros((STEP, 8, 128), F32)
        other = jnp.full((STEP, 8, 128), -1, I32)
        for r in range(8 * h, 8 * h + 8):
            value = ids[r, 0:STEP]
            matched = value == own[h]
            own_sum += jnp.where(matched, 1.0, 0.0)
            other = jnp.maximum(other, jnp.where(matched, -1, value))
        own_sum = jnp.sum(own_sum, axis=0)
        counts.append((own_sum, float(8 * STEP) - own_sum))
        others.append(spread(jnp.max(other, axis=0)[7:8]))
    encode(jnp.where(lane >= 120, others[0], jnp.where(lane < 8, pltpu.roll(others[1], 8, 1), -1))[0:1], 4)

    def start_a(n, table):
        part[n] = table.reshape(2, 16, 128)
        for slot, flip, peer in a_peers:
            pltpu.make_async_remote_copy(
                src_ref=part.at[n, 1 - core if flip else core], dst_ref=part_in.at[n, slot],
                send_sem=a_send.at[n], recv_sem=a_recv.at[n], device_id=peer, device_id_type=MESH,
            ).start()

    def start_b(n):
        drain(part_in.at[n, pl.ds(1, 7)], a_recv.at[n])
        total = part[n, core]
        for slot in range(1, 8):
            total += part_in[n, slot]
        half[n] = total
        for i, peer in b_peers:
            pltpu.make_async_remote_copy(
                src_ref=half.at[n], dst_ref=half_in.at[n, i],
                send_sem=b_send.at[n], recv_sem=b_recv.at[n], device_id=peer, device_id_type=MESH,
            ).start()

    def finish_b(n):
        drain(half_in.at[n], b_recv.at[n])
        total = half[n]
        for i in range(15):
            total += half_in[n, i]
        return total

    def share(n, factor):
        factors[n, core] = factor
        pltpu.make_async_remote_copy(
            src_ref=factors.at[n, core], dst_ref=factors.at[n, core],
            send_sem=c_send.at[n], recv_sem=c_recv.at[n], device_id=partner, device_id_type=MESH,
        ).start()
        drain(factors.at[n, 1 - core], c_recv.at[n])
        return factors[n].reshape(32, 128)

    start_a(0, scatter(counts))

    def fill_halo(depth, get, put, row_in, col_in, corner_in):
        east = pltpu.roll(col_in[0], 120, 1)
        west = col_in[1]
        for k in range(1, depth + 1):
            both = jnp.where(q < 4, spread(west[8 - k : 9 - k]), spread(east[k - 1 : k]))
            for r in range(STEP):
                put(r, 15 + k, pltpu.roll(both, (128 - 8 * r) % 128, 1) if r else both)

        def mirrored(j, t, value):
            return jnp.where(mirror_top, get(j - 1, t), jnp.where(mirror_bottom, get(STEP - j, t), value))

        q_wide = lax.broadcasted_iota(I32, (8, COLS), 0)
        for j in range(1, depth + 1):
            wide = jnp.where(
                q_wide < 4,
                spread(row_in[0, 8 - j : 9 - j, :], (8, COLS)),
                spread(row_in[1, j - 1 : j, :], (8, COLS)),
            )
            rows = jnp.concatenate([wide[:, tile(t)] for t in range(TILES)], axis=0)
            for t, value in enumerate(turned(rows, j % 4)):
                put(15 + j, t, mirrored(j, t, value))
        for k in range(1, depth):
            near, far = jnp.full((8, 128), k - 1, I32), jnp.full((8, 128), 128 - k, I32)
            north = jnp.where(lane < 64, pick(corner_in[1], far), pick(corner_in[0], near))
            south = jnp.where(lane < 64, pick(corner_in[3], far), pick(corner_in[2], near))
            for j in range(1, depth + 1 - k):
                value = jnp.where(s < 4, spread(north[8 - j : 9 - j]), spread(south[j - 1 : j]))
                put(15 + j, 15 + k, mirrored(j, 15 + k, value))

    def sweeper(src, dst):
        def get(row, a, b):
            return level[src, row, a:b]

        def vertical(row, a, b):
            if row == 0:
                north = jnp.where(s == 0, get(STEP, a, b), pltpu.roll(get(STEP - 1, a, b), 1, 2))
                return north + get(1, a, b)
            if row == STEP - 1:
                south = jnp.where(s == 7, get(STEP, a, b), pltpu.roll(get(0, a, b), 127, 2))
                return get(STEP - 2, a, b) + south
            if row == STEP:
                return jnp.where(s < 4, get(0, a, b), get(STEP - 1, a, b)) + get(STEP + 1, a, b)
            return get(row - 1, a, b) + get(row + 1, a, b)

        def west_edge(row):
            value = pltpu.roll(level[src, row, STEP - 1], 1, 0)
            return jnp.where(q == 0, jnp.where(lane < 8, level[src, row, STEP], pltpu.roll(value, 8, 1)), value)[None]

        def east_edge(row):
            value = pltpu.roll(level[src, row, 0], 7, 0)
            return jnp.where(q == 7, jnp.where(lane >= 120, level[src, row, STEP], pltpu.roll(value, 120, 1)), value)[None]

        def span(row, a, b):
            lo, hi = max(a - 1, 0), min(b + 1, STEP)
            values = get(row, lo, hi)
            centre = values[a - lo : b - lo]
            west = [values[0 : b - 1 - lo]] if b - 1 > lo else []
            east = [values[a + 1 - lo :]] if a + 1 < hi else []
            west = jnp.concatenate(west if a > 0 else [west_edge(row)] + west, axis=0)
            east = jnp.concatenate(east if b < STEP else east + [east_edge(row)], axis=0)
            level[dst, row, a:b] = (centre + vertical(row, a, b)) + (west + east)

        def beyond(row, count):
            for k in range(1, count + 1):
                if k == 1:
                    inward = jnp.where(q < 4, level[src, row, 0], level[src, row, STEP - 1])[None]
                else:
                    inward = get(row, 14 + k, 15 + k)
                outward = get(row, 16 + k, 17 + k)
                at = (15 + k, 16 + k)
                level[dst, row, at[0] : at[1]] = (get(row, *at) + vertical(row, *at)) + (inward + outward)

        return span, beyond

    def outer_rows(beyond, span, left):
        for row in range(STEP):
            beyond(row, left)
        for j in range(1, left + 1):
            span(15 + j, 0, STEP)
            beyond(15 + j, left - j)

    for n in range(1, SWEEPS + 1):
        span, _ = sweeper(n - 1, n)
        for row in range(n, STEP - n):
            span(row, n, STEP - n)

    def put_prior(row, t, value):
        level[0, row, t] = value

    for ref, m in ((prow, 0), (pcol, 1), (pcorner, 2)):
        drain(ref, halo_recv.at[m])
    fill_halo(DEPTH, lambda row, t: level[0, row, t], put_prior, prow, pcol, pcorner)
    for n in range(1, SWEEPS + 1):
        span, beyond = sweeper(n - 1, n)
        for row in range(STEP):
            if n <= row < STEP - n:
                span(row, 0, n)
                span(row, STEP - n, STEP)
            else:
                span(row, 0, STEP)
        outer_rows(beyond, span, DEPTH - n)

    start_b(0)
    start_a(1, scatter([block_sums(SWEEPS, h) for h in range(2)]))

    def put_ids(row, t, value):
        ids[row, t] = value

    for ref, m in ((zrow, 0), (zcol, 1), (zcorner, 2)):
        drain(ref, zhalo_recv.at[m])
    fill_halo(IDS, lambda row, t: ids[row, t], put_ids, zrow, zcol, zcorner)

    def beside_ids(cells, own_cells):
        other = jnp.full((8, 128), -1, I32)
        for row, t in cells:
            value = ids[row, t]
            other = jnp.maximum(other, jnp.where(value == own_cells, -1, value))
        return jnp.where(lane[0:1] < 64, other[0:1], other[7:8])

    for h in range(2):
        cells = [(row, 15 + k) for row in range(8 * h, 8 * h + 8) for k in range(1, IDS + 1)]
        encode(beside_ids(cells, own[h]), 5 + h)
    lines, cells = own_ids(STEP)
    own.append(cells)
    encode(lines[0], 7)
    encode(lines[1], 8)
    corner = beside_ids([(15 + j, 15 + k) for j in range(1, IDS) for k in range(1, IDS + 1 - j)], own[2])
    encode(corner, 9)

    start_b(1)
    rate_copy.wait()
    target = rate_in[core] * finish_b(0)

    def lookup(table, groups):
        rows = jnp.dot(split2(table), onehot_lo[:, 0 : 128 * groups], preferred_element_type=F32)
        rows = rows[0:32] + rows[32:64]
        lines = []
        for g in range(groups):
            lines.append(spread(jnp.sum(rows[:, 128 * g : 128 * g + 128] * onehot_hi[g], axis=0, keepdims=True)))
        return lines

    def cell_factors(near, far, ext):
        mine = jnp.where(q < 4, near, far)
        next_block = jnp.where(lane >= 120, ext, pltpu.roll(near, 120, 1))
        return mine, jnp.where(q < 4, far, next_block)

    def factors_of(lines):
        ext = lines[4]
        return [cell_factors(lines[0], lines[1], ext), cell_factors(lines[2], lines[3], pltpu.roll(ext, 120, 1))]

    lines = lookup(share(0, target / finish_b(1)), GROUPS)
    pairs = factors_of(lines) + [cell_factors(lines[7], lines[8], lines[9])]
    sides = [lines[5], lines[6], lines[9]]
    for row in range(STEP + IDS):
        h = row // 8
        mine, east = pairs[h]
        scale = jnp.where(ids[row, 0:STEP] == own[h], mine, east)
        level[SWEEPS, row, 0:STEP] = level[SWEEPS, row, 0:STEP] * scale
        left = IDS if row < STEP else IDS - (row - 15)
        if left:
            reach = slice(STEP, STEP + left)
            scale = jnp.where(ids[row, reach] == own[h], mine, sides[h])
            level[SWEEPS, row, reach] = level[SWEEPS, row, reach] * scale

    for n in range(1, SWEEPS + 1):
        span, beyond = sweeper((n + 2) % 4, (n + 3) % 4)
        for row in range(STEP):
            span(row, 0, STEP)
        outer_rows(beyond, span, SWEEPS - n)

    start_a(2, scatter([block_sums(2, h) for h in range(2)]))
    start_b(2)
    pairs = factors_of(lookup(share(1, target / finish_b(2)), 5))
    for r in range(STEP):
        mine, east = pairs[r // 8]
        slot = r % 4
        for t in range(STEP):
            scale = jnp.where(ids[r, t] == own[r // 8], mine, east)
            turn.at[slot][pl.ds(t, 8, stride=STEP), :] = level[2, r, t] * scale
        rows = turn[slot].T
        for t in range(TILES):
            pin.at[t][pl.ds(r, 8, stride=STEP), :] = rows[8 * t : 8 * t + 8]
    for t in range(TILES):
        pltpu.make_async_copy(pin.at[t], out.at[:, tile(t)], store_sem).start()

    for sems, shapes in ((halo_send, (prow, pcol, pcorner)), (zhalo_send, (zrow, zcol, zcorner))):
        for m, ref in enumerate(shapes):
            drain(ref, sems.at[m])
    for n in range(3):
        drain(part_in.at[n, pl.ds(1, 7)], a_send.at[n])
        drain(half_in.at[n], b_send.at[n])
    for n in range(2):
        drain(factors.at[n, core], c_send.at[n])
    drain(pin, store_sem)


def body(prior, zone_ids, rate):
    dma = pltpu.SemaphoreType.DMA
    vmem = pltpu.VMEM
    anywhere = pl.BlockSpec(memory_space=pl.ANY)
    return pl.pallas_call(
        kernel,
        out_shape=jax.ShapeDtypeStruct((ROWS, COLS), F32),
        in_specs=[anywhere, anywhere, anywhere],
        out_specs=anywhere,
        scratch_shapes=[
            vmem((TILES, ROWS, 128), F32),
            vmem((TILES, ROWS, 128), I32),
            vmem((4, 128, 128), F32),
            vmem((4, 128, 128), I32),
            vmem((4, SIDE, SIDE, 8, 128), F32),
            vmem((STEP + IDS, STEP + IDS, 8, 128), I32),
            vmem((2, 8, COLS), F32),
            vmem((2, 8, 128), F32),
            vmem((4, 8, 128), F32),
            vmem((2, 8, COLS), I32),
            vmem((2, 8, 128), I32),
            vmem((4, 8, 128), I32),
            vmem((2, 8, 128), F32),
            vmem((2, 8, 128), I32),
            vmem((GROUPS, 32, 128), F32),
            vmem((128, 128 * GROUPS), BF16),
            vmem((3, 2, 16, 128), F32),
            vmem((3, 8, 16, 128), F32),
            vmem((3, 16, 128), F32),
            vmem((3, 15, 16, 128), F32),
            vmem((2, 2, 16, 128), F32),
            dma((2, 3)),
            dma,
            dma,
            dma((3,)),
            dma((3,)),
            dma((3,)),
            dma((3,)),
            dma((3,)),
            dma((3,)),
            dma((3,)),
            dma((3,)),
            dma((2,)),
            dma((2,)),
            vmem((2, 16, 128), F32),
        ],
        compiler_params=pltpu.CompilerParams(collective_id=0, has_side_effects=True),
    )(prior, zone_ids, rate.reshape(2, 16, 128))


def solution(mesh):
    placed = (P("lat", "lon"), P("lat", "lon"), P())
    return jax.shard_map(
        body, mesh=mesh, in_specs=placed, out_specs=P("lat", "lon"), check_vma=False
    )
```

profile of v0, /device:TPU:1, one launch (start us, length us, event | category | flops | bytes accessed | tf_op | source)
XLA Modules:
  0.0 39.2 jit_solution(14634965833763631628)
XLA Ops:
  0.0 36.9 %shard_map.37 = f32[128,2048]{1,0:T(8,128)} custom-call(f32[128,2048]{1,0:T(8,128)} %prior.1, s32[128,2048]{1,0:T(8,128)} %zones.1, f32[2,16,128]{2,1,0:T(8,128)} %bitcast.1), custom_call_target="tpu_custom_call" | custom-call | tf_op jit(solution)/shard_map/pallas_call | solution.py:466
  36.9 2.3 %copy.5 = f32[128,2048]{1,0:T(8,128)} copy(f32[128,2048]{1,0:T(8,128)} %shard_map.37) | data formatting | bytes 2097152
where the time goes:
time: 39.4 us; the launch traced here: 39.2 us
  Pallas kernels  36.9 us (94%)
  local copies, waits for them, and re-layouts  2.3 us (6%)
    pallas_call x1, Pallas kernels, body(): pl.pallas_call(kernel, out_shape=jax.ShapeDtypeStruct((ROWS, COLS), F32),...  36.9 us
    unnamed x1, local copies, waits for them, and re-layouts  2.3 us

commit v1 on v0

--- a/solution.py
+++ b/solution.py
@@ -13,6 +13,7 @@
 IDS = 3
 SIDE = STEP + DEPTH
 GROUPS = 10
+VMEM_LIMIT = 55200000
 MESH = pl.DeviceIdType.MESH
 F32, I32, BF16 = jnp.float32, jnp.int32, jnp.bfloat16
 
@@ -24,11 +25,11 @@
 
 
 def place(row, col):
-    return {"lat": lax.rem(row + 8, 8), "lon": lax.rem(col + 16, 16)}
+    return {"lat": jnp.bitwise_and(row, 7), "lon": jnp.bitwise_and(col, 15)}
 
 
 def device(x, core, y, z):
-    return (lax.rem(x, 4) * 2 + core, lax.rem(y, 4) * 4 + lax.rem(z, 4))
+    return (jnp.bitwise_and(x, 3) * 2 + core, jnp.bitwise_and(y, 3) * 4 + jnp.bitwise_and(z, 3))
 
 
 FAR_A = [2, 3, 1, 0]
@@ -43,24 +44,25 @@
 
 
 def kernel(
-    prior, zones, rate, out,
-    pin, zin, turn, iturn, level, ids,
+    prior, zones, rate, final,
+    pin, zin, turn, iturn, level0, level1, level2, level3, ids,
     prow, pcol, pcorner, zrow, zcol, zcorner, ppack, zpack,
     onehot_hi, onehot_lo,
     part, part_in, half, half_in, factors,
-    load_sem, store_sem, rate_sem, halo_send, halo_recv, zhalo_send, zhalo_recv,
+    load_sem, rate_sem, halo_send, halo_recv, zhalo_send, zhalo_recv,
     a_send, a_recv, b_send, b_recv, c_send, c_recv, rate_in,
 ):
+    level = [level0, level1, level2, level3]
     lat, lon = lax.axis_index("lat"), lax.axis_index("lon")
-    x, core = lax.div(lat, 2), lax.rem(lat, 2)
-    y, z = lax.div(lon, 4), lax.rem(lon, 4)
+    x, core = jnp.right_shift(lat, 1), jnp.bitwise_and(lat, 1)
+    y, z = jnp.right_shift(lon, 2), jnp.bitwise_and(lon, 3)
 
     around = [(-1, 0), (1, 0), (0, -1), (0, 1), (-1, -1), (-1, 1), (1, -1), (1, 1)]
     a_peers = []
     for d in FAR_A:
         for flip in (1, 0):
             if (d, flip) != (0, 0):
-                a_peers.append((d * 2 + flip, flip, device(x + d, jnp.where(flip == 1, 1 - core, core), y, z)))
+                a_peers.append((d * 2 + flip, flip, device(x + d, 1 - core if flip else core, y, z)))
     b_peers = [(i, device(x, core, y + a, z + b)) for i, (a, b) in enumerate(FAR_B)]
     partner = device(x, 1 - core, y, z)
 
@@ -124,12 +126,12 @@
         send(packed.at[0], col_in.at[0], out_sem.at[1], in_sem.at[1], 0, -1)
         send(packed.at[1], col_in.at[1], out_sem.at[1], in_sem.at[1], 0, 1)
 
+    pl.semaphore_wait(barrier, greeted)
+    send_rows(prior, prow, pcorner, halo_send, halo_recv)
     drain(pin.at[0], load_sem.at[0, 0])
     drain(pin.at[TILES - 1], load_sem.at[0, 1])
     pack(pin, ppack)
-    pl.semaphore_wait(barrier, greeted)
     send_cols(ppack, pcol, halo_send, halo_recv)
-    send_rows(prior, prow, pcorner, halo_send, halo_recv)
     drain(zin.at[0], load_sem.at[1, 0])
     drain(zin.at[TILES - 1], load_sem.at[1, 1])
     pack(zin, zpack)
@@ -150,7 +152,7 @@
                 write(r, t, value)
 
     def write_prior(r, t, value):
-        level[0, r, t] = value
+        level0[r, t] = value
 
     def write_ids(r, t, value):
         ids[r, t] = value
@@ -202,11 +204,11 @@
         )
         return table[0:32] + table[32:64]
 
-    def block_sums(n, h):
+    def block_sums(source, h):
         own_sum, east_sum = jnp.zeros((STEP, 8, 128), F32), jnp.zeros((STEP, 8, 128), F32)
         for r in range(8 * h, 8 * h + 8):
             matched = ids[r, 0:STEP] == own[h]
-            value = level[n, r, 0:STEP]
+            value = source[r, 0:STEP]
             own_sum += jnp.where(matched, value, 0.0)
             east_sum += jnp.where(matched, 0.0, value)
         return jnp.sum(own_sum, axis=0), jnp.sum(east_sum, axis=0)
@@ -263,17 +265,26 @@
 
     start_a(0, scatter(counts))
 
-    def fill_halo(depth, get, put, row_in, col_in, corner_in):
+    def fill_halo(depth, get, put, row_in, col_in, corner_in, sems):
+        def mirrored(j, t, value):
+            return jnp.where(mirror_top, get(j - 1, t), jnp.where(mirror_bottom, get(STEP - j, t), value))
+
+        drain(col_in, sems.at[1])
         east = pltpu.roll(col_in[0], 120, 1)
         west = col_in[1]
         for k in range(1, depth + 1):
             both = jnp.where(q < 4, spread(west[8 - k : 9 - k]), spread(east[k - 1 : k]))
             for r in range(STEP):
                 put(r, 15 + k, pltpu.roll(both, (128 - 8 * r) % 128, 1) if r else both)
-
-        def mirrored(j, t, value):
-            return jnp.where(mirror_top, get(j - 1, t), jnp.where(mirror_bottom, get(STEP - j, t), value))
-
+        drain(corner_in, sems.at[2])
+        for k in range(1, depth):
+            near, far = jnp.full((8, 128), k - 1, I32), jnp.full((8, 128), 128 - k, I32)
+            north = jnp.where(lane < 64, pick(corner_in[1], far), pick(corner_in[0], near))
+            south = jnp.where(lane < 64, pick(corner_in[3], far), pick(corner_in[2], near))
+            for j in range(1, depth + 1 - k):
+                value = jnp.where(s < 4, spread(north[8 - j : 9 - j]), spread(south[j - 1 : j]))
+                put(15 + j, 15 + k, mirrored(j, 15 + k, value))
+        drain(row_in, sems.at[0])
         q_wide = lax.broadcasted_iota(I32, (8, COLS), 0)
         for j in range(1, depth + 1):
             wide = jnp.where(
@@ -284,17 +295,10 @@
             rows = jnp.concatenate([wide[:, tile(t)] for t in range(TILES)], axis=0)
             for t, value in enumerate(turned(rows, j % 4)):
                 put(15 + j, t, mirrored(j, t, value))
-        for k in range(1, depth):
-            near, far = jnp.full((8, 128), k - 1, I32), jnp.full((8, 128), 128 - k, I32)
-            north = jnp.where(lane < 64, pick(corner_in[1], far), pick(corner_in[0], near))
-            south = jnp.where(lane < 64, pick(corner_in[3], far), pick(corner_in[2], near))
-            for j in range(1, depth + 1 - k):
-                value = jnp.where(s < 4, spread(north[8 - j : 9 - j]), spread(south[j - 1 : j]))
-                put(15 + j, 15 + k, mirrored(j, 15 + k, value))
 
     def sweeper(src, dst):
         def get(row, a, b):
-            return level[src, row, a:b]
+            return src[row, a:b]
 
         def vertical(row, a, b):
             if row == 0:
@@ -308,12 +312,12 @@
             return get(row - 1, a, b) + get(row + 1, a, b)
 
         def west_edge(row):
-            value = pltpu.roll(level[src, row, STEP - 1], 1, 0)
-            return jnp.where(q == 0, jnp.where(lane < 8, level[src, row, STEP], pltpu.roll(value, 8, 1)), value)[None]
+            value = pltpu.roll(src[row, STEP - 1], 1, 0)
+            return jnp.where(q == 0, jnp.where(lane < 8, src[row, STEP], pltpu.roll(value, 8, 1)), value)[None]
 
         def east_edge(row):
-            value = pltpu.roll(level[src, row, 0], 7, 0)
-            return jnp.where(q == 7, jnp.where(lane >= 120, level[src, row, STEP], pltpu.roll(value, 120, 1)), value)[None]
+            value = pltpu.roll(src[row, 0], 7, 0)
+            return jnp.where(q == 7, jnp.where(lane >= 120, src[row, STEP], pltpu.roll(value, 120, 1)), value)[None]
 
         def span(row, a, b):
             lo, hi = max(a - 1, 0), min(b + 1, STEP)
@@ -323,17 +327,17 @@
             east = [values[a + 1 - lo :]] if a + 1 < hi else []
             west = jnp.concatenate(west if a > 0 else [west_edge(row)] + west, axis=0)
             east = jnp.concatenate(east if b < STEP else east + [east_edge(row)], axis=0)
-            level[dst, row, a:b] = (centre + vertical(row, a, b)) + (west + east)
+            dst[row, a:b] = (centre + vertical(row, a, b)) + (west + east)
 
         def beyond(row, count):
             for k in range(1, count + 1):
                 if k == 1:
-                    inward = jnp.where(q < 4, level[src, row, 0], level[src, row, STEP - 1])[None]
+                    inward = jnp.where(q < 4, src[row, 0], src[row, STEP - 1])[None]
                 else:
                     inward = get(row, 14 + k, 15 + k)
                 outward = get(row, 16 + k, 17 + k)
                 at = (15 + k, 16 + k)
-                level[dst, row, at[0] : at[1]] = (get(row, *at) + vertical(row, *at)) + (inward + outward)
+                dst[row, at[0] : at[1]] = (get(row, *at) + vertical(row, *at)) + (inward + outward)
 
         return span, beyond
 
@@ -345,18 +349,16 @@
             beyond(15 + j, left - j)
 
     for n in range(1, SWEEPS + 1):
-        span, _ = sweeper(n - 1, n)
+        span, _ = sweeper(level[n - 1], level[n])
         for row in range(n, STEP - n):
             span(row, n, STEP - n)
 
     def put_prior(row, t, value):
-        level[0, row, t] = value
-
-    for ref, m in ((prow, 0), (pcol, 1), (pcorner, 2)):
-        drain(ref, halo_recv.at[m])
-    fill_halo(DEPTH, lambda row, t: level[0, row, t], put_prior, prow, pcol, pcorner)
+        level0[row, t] = value
+
+    fill_halo(DEPTH, lambda row, t: level0[row, t], put_prior, prow, pcol, pcorner, halo_recv)
     for n in range(1, SWEEPS + 1):
-        span, beyond = sweeper(n - 1, n)
+        span, beyond = sweeper(level[n - 1], level[n])
         for row in range(STEP):
             if n <= row < STEP - n:
                 span(row, 0, n)
@@ -365,15 +367,13 @@
                 span(row, 0, STEP)
         outer_rows(beyond, span, DEPTH - n)
 
+    start_a(1, scatter([block_sums(level3, h) for h in range(2)]))
     start_b(0)
-    start_a(1, scatter([block_sums(SWEEPS, h) for h in range(2)]))
 
     def put_ids(row, t, value):
         ids[row, t] = value
 
-    for ref, m in ((zrow, 0), (zcol, 1), (zcorner, 2)):
-        drain(ref, zhalo_recv.at[m])
-    fill_halo(IDS, lambda row, t: ids[row, t], put_ids, zrow, zcol, zcorner)
+    fill_halo(IDS, lambda row, t: ids[row, t], put_ids, zrow, zcol, zcorner, zhalo_recv)
 
     def beside_ids(cells, own_cells):
         other = jnp.full((8, 128), -1, I32)
@@ -420,33 +420,25 @@
         h = row // 8
         mine, east = pairs[h]
         scale = jnp.where(ids[row, 0:STEP] == own[h], mine, east)
-        level[SWEEPS, row, 0:STEP] = level[SWEEPS, row, 0:STEP] * scale
+        level3[row, 0:STEP] = level3[row, 0:STEP] * scale
         left = IDS if row < STEP else IDS - (row - 15)
         if left:
             reach = slice(STEP, STEP + left)
             scale = jnp.where(ids[row, reach] == own[h], mine, sides[h])
-            level[SWEEPS, row, reach] = level[SWEEPS, row, reach] * scale
+            level3[row, reach] = level3[row, reach] * scale
 
     for n in range(1, SWEEPS + 1):
-        span, beyond = sweeper((n + 2) % 4, (n + 3) % 4)
+        span, beyond = sweeper(level[(n + 2) % 4], level[n - 1] if n < SWEEPS else final)
         for row in range(STEP):
             span(row, 0, STEP)
         outer_rows(beyond, span, SWEEPS - n)
 
-    start_a(2, scatter([block_sums(2, h) for h in range(2)]))
+    start_a(2, scatter([block_sums(final, h) for h in range(2)]))
     start_b(2)
     pairs = factors_of(lookup(share(1, target / finish_b(2)), 5))
     for r in range(STEP):
         mine, east = pairs[r // 8]
-        slot = r % 4
-        for t in range(STEP):
-            scale = jnp.where(ids[r, t] == own[r // 8], mine, east)
-            turn.at[slot][pl.ds(t, 8, stride=STEP), :] = level[2, r, t] * scale
-        rows = turn[slot].T
-        for t in range(TILES):
-            pin.at[t][pl.ds(r, 8, stride=STEP), :] = rows[8 * t : 8 * t + 8]
-    for t in range(TILES):
-        pltpu.make_async_copy(pin.at[t], out.at[:, tile(t)], store_sem).start()
+        final[r] = final[r] * jnp.where(ids[r, 0:STEP] == own[r // 8], mine, east)
 
     for sems, shapes in ((halo_send, (prow, pcol, pcorner)), (zhalo_send, (zrow, zcol, zcorner))):
         for m, ref in enumerate(shapes):
@@ -456,24 +448,45 @@
         drain(half_in.at[n], b_send.at[n])
     for n in range(2):
         drain(factors.at[n, core], c_send.at[n])
-    drain(pin, store_sem)
+
+
+def finish(final, out, turn, pout, store_sem):
+    for h in range(2):
+        for r in range(8 * h, 8 * h + 8):
+            slot = r % 4
+            for t in range(STEP):
+                turn.at[slot][pl.ds(t, 8, stride=STEP), :] = final[r, t]
+            rows = turn[slot].T
+            for t in range(TILES):
+                pout.at[t][pl.ds(r, 8, stride=STEP), :] = rows[8 * t : 8 * t + 8]
+        for t in range(TILES):
+            pltpu.make_async_copy(
+                pout.at[t].reshape(8, STEP, 128).at[:, 8 * h : 8 * h + 8, :],
+                out.reshape(8, STEP, COLS).at[:, 8 * h : 8 * h + 8, 128 * t : 128 * t + 128],
+                store_sem,
+            ).start()
+    drain(pout, store_sem)
 
 
 def body(prior, zone_ids, rate):
     dma = pltpu.SemaphoreType.DMA
     vmem = pltpu.VMEM
-    anywhere = pl.BlockSpec(memory_space=pl.ANY)
-    return pl.pallas_call(
+    outside = pl.BlockSpec(memory_space=pltpu.HBM)
+    inside = pl.BlockSpec(memory_space=pltpu.VMEM)
+    scaled = pl.pallas_call(
         kernel,
-        out_shape=jax.ShapeDtypeStruct((ROWS, COLS), F32),
-        in_specs=[anywhere, anywhere, anywhere],
-        out_specs=anywhere,
+        out_shape=jax.ShapeDtypeStruct((STEP, STEP, 8, 128), F32),
+        in_specs=[outside] * 3,
+        out_specs=inside,
         scratch_shapes=[
             vmem((TILES, ROWS, 128), F32),
             vmem((TILES, ROWS, 128), I32),
             vmem((4, 128, 128), F32),
             vmem((4, 128, 128), I32),
-            vmem((4, SIDE, SIDE, 8, 128), F32),
+            vmem((SIDE, SIDE, 8, 128), F32),
+            vmem((SIDE, SIDE, 8, 128), F32),
+            vmem((SIDE, SIDE, 8, 128), F32),
+            vmem((SIDE, SIDE, 8, 128), F32),
             vmem((STEP + IDS, STEP + IDS, 8, 128), I32),
             vmem((2, 8, COLS), F32),
             vmem((2, 8, 128), F32),
@@ -492,7 +505,6 @@
             vmem((2, 2, 16, 128), F32),
             dma((2, 3)),
             dma,
-            dma,
             dma((3,)),
             dma((3,)),
             dma((3,)),
@@ -505,8 +517,18 @@
             dma((2,)),
             vmem((2, 16, 128), F32),
         ],
-        compiler_params=pltpu.CompilerParams(collective_id=0, has_side_effects=True),
+        compiler_params=pltpu.CompilerParams(
+            collective_id=0, has_side_effects=True, vmem_limit_bytes=VMEM_LIMIT
+        ),
     )(prior, zone_ids, rate.reshape(2, 16, 128))
+    return pl.pallas_call(
+        finish,
+        out_shape=jax.ShapeDtypeStruct((ROWS, COLS), F32),
+        in_specs=[inside],
+        out_specs=outside,
+        scratch_shapes=[vmem((4, 128, 128), F32), vmem((TILES, ROWS, 128), F32), dma],
+        compiler_params=pltpu.CompilerParams(vmem_limit_bytes=32 * 1024 * 1024),
+    )(scaled)
 
 
 def solution(mesh):

time: 39.4 us -> 37 us (0.939)
  local copies, waits for them, and re-layouts: 2.3 us -> 0.72 us
  Pallas kernels: 36.9 us -> 36.1 us
    unnamed x1 -> x2, local copies, waits for them, and re-layouts: 2.3 us -> 0.72 us
    pallas_call x1 -> x2, Pallas kernels: 36.9 us -> 36.1 us  [the longest x1 34.6 us: body(): pl.pallas_call(kernel, out_shape=jax.ShapeDtypeStruct((STEP, STEP, 8, 128...]
where the time goes in v1:
time: 37 us; the launch traced here: 36.8 us
  Pallas kernels  36.1 us (98%)
  local copies, waits for them, and re-layouts  0.72 us (2%)
    pallas_call x1, Pallas kernels, body(): pl.pallas_call(kernel, out_shape=jax.ShapeDtypeStruct((STEP, STEP, 8, 128...  34.6 us
    pallas_call x1, Pallas kernels, body(): pl.pallas_call(finish, out_shape=jax.ShapeDtypeStruct((ROWS, COLS), F32),...  1.48 us

profile of v1, /device:TPU:1, one launch (start us, length us, event | category | flops | bytes accessed | tf_op | source)
XLA Modules:
  0.0 36.8 jit_solution(5550732590794335279)
XLA Ops:
  0.0 0.0 copy-start
  0.0 0.7 %copy-done = f32[4096]{0:T(1024)S(1)} copy-done((f32[4096]{0:T(1024)S(1)}, f32[4096]{0:T(1024)}, u32[]{:S(2)}) %copy-start) | copy-done | bytes 16408
  0.7 34.6 %shard_map.37.final = f32[16,16,8,128]{3,2,1,0:T(8,128)S(1)} custom-call(f32[128,2048]{1,0:T(8,128)} %prior.1, s32[128,2048]{1,0:T(8,128)} %zones.1, f32[2,16,128]{2,1,0:T(8,128)S(1)} %bitcast.1), custom_call_target="tpu_custom_call" | custom-call | tf_op jit(solution)/shard_map/pallas_call | solution.py:476
  35.3 1.5 %shard_map.38 = f32[128,2048]{1,0:T(8,128)} custom-call(f32[16,16,8,128]{3,2,1,0:T(8,128)S(1)} %shard_map.37.final), custom_call_target="tpu_custom_call" | custom-call | tf_op jit(solution)/shard_map/pallas_call | solution.py:524
Async XLA Ops:
  0.0 0.7 %copy-start = (f32[4096]{0:T(1024)S(1)}, f32[4096]{0:T(1024)}, u32[]{:S(2)}) copy-start(f32[4096]{0:T(1024)} %param.5) | copy-start | bytes 49156

commit v2 on v1

--- a/solution.py
+++ b/solution.py
@@ -44,8 +44,8 @@
 
 
 def kernel(
-    prior, zones, rate, final,
-    pin, zin, turn, iturn, level0, level1, level2, level3, ids,
+    prior, zones, rate, signed, scales,
+    pin, zin, turn, iturn, level0, level1, level2, level3, final, ids,
     prow, pcol, pcorner, zrow, zcol, zcorner, ppack, zpack,
     onehot_hi, onehot_lo,
     part, part_in, half, half_in, factors,
@@ -68,8 +68,8 @@
 
     barrier = pltpu.get_barrier_semaphore()
     greeted = 0
-    for dr, dc in around:
-        pl.semaphore_signal(barrier, inc=1, device_id=place(lat + dr, lon + dc), device_id_type=MESH)
+    for peer in [peer for _, peer in b_peers] + [peer for _, _, peer in a_peers] + [place(lat + dr, lon + dc) for dr, dc in around]:
+        pl.semaphore_signal(barrier, inc=1, device_id=peer, device_id_type=MESH)
         greeted += 1
 
     def tile(t):
@@ -81,13 +81,6 @@
     rate_copy = pltpu.make_async_copy(rate, rate_in, rate_sem)
     rate_copy.start()
 
-    for _, _, peer in a_peers:
-        pl.semaphore_signal(barrier, inc=1, device_id=peer, device_id_type=MESH)
-        greeted += 1
-    for _, peer in b_peers:
-        pl.semaphore_signal(barrier, inc=1, device_id=peer, device_id_type=MESH)
-        greeted += 1
-
     lane = lax.broadcasted_iota(I32, (8, 128), 1)
     q = lax.broadcasted_iota(I32, (8, 128), 0)
     s = lax.rem(lane, 8)
@@ -100,13 +93,14 @@
     def spread(row, shape=(8, 128)):
         return jnp.broadcast_to(row, shape)
 
+    inner = pl.ds(1, TILES - 2)
+
     def pack(ref, packed):
         index = 16 * s + lax.div(lane, 8)
         packed[0] = pick(ref[0].T[0:8], index)
         packed[1] = pick(ref[TILES - 1].T[120:128], index)
 
     first8, last8 = pl.ds(0, 8), pl.ds(ROWS - 8, 8)
-    first128, last128 = pl.ds(0, 128), pl.ds(COLS - 128, 128)
 
     def send(src, dst, send_sem, recv_sem, dr, dc):
         pltpu.make_async_remote_copy(
@@ -115,30 +109,24 @@
         ).start()
 
     def send_rows(source, row_in, corner_in, out_sem, in_sem):
-        send(source.at[first8, first128], corner_in.at[2], out_sem.at[2], in_sem.at[2], -1, -1)
-        send(source.at[first8, last128], corner_in.at[3], out_sem.at[2], in_sem.at[2], -1, 1)
-        send(source.at[last8, first128], corner_in.at[0], out_sem.at[2], in_sem.at[2], 1, -1)
-        send(source.at[last8, last128], corner_in.at[1], out_sem.at[2], in_sem.at[2], 1, 1)
-        send(source.at[first8, :], row_in.at[1], out_sem.at[0], in_sem.at[0], -1, 0)
-        send(source.at[last8, :], row_in.at[0], out_sem.at[0], in_sem.at[0], 1, 0)
+        send(source.at[:, first8, :], row_in.at[1], out_sem.at[0], in_sem.at[0], -1, 0)
+        send(source.at[:, last8, :], row_in.at[0], out_sem.at[0], in_sem.at[0], 1, 0)
+        send(source.at[0, first8, :], corner_in.at[2], out_sem.at[2], in_sem.at[2], -1, -1)
+        send(source.at[TILES - 1, first8, :], corner_in.at[3], out_sem.at[2], in_sem.at[2], -1, 1)
+        send(source.at[0, last8, :], corner_in.at[0], out_sem.at[2], in_sem.at[2], 1, -1)
+        send(source.at[TILES - 1, last8, :], corner_in.at[1], out_sem.at[2], in_sem.at[2], 1, 1)
 
     def send_cols(packed, col_in, out_sem, in_sem):
         send(packed.at[0], col_in.at[0], out_sem.at[1], in_sem.at[1], 0, -1)
         send(packed.at[1], col_in.at[1], out_sem.at[1], in_sem.at[1], 0, 1)
 
-    pl.semaphore_wait(barrier, greeted)
-    send_rows(prior, prow, pcorner, halo_send, halo_recv)
     drain(pin.at[0], load_sem.at[0, 0])
     drain(pin.at[TILES - 1], load_sem.at[0, 1])
     pack(pin, ppack)
+    drain(pin.at[inner], load_sem.at[0, 2])
+    pl.semaphore_wait(barrier, greeted)
+    send_rows(pin, prow, pcorner, halo_send, halo_recv)
     send_cols(ppack, pcol, halo_send, halo_recv)
-    drain(zin.at[0], load_sem.at[1, 0])
-    drain(zin.at[TILES - 1], load_sem.at[1, 1])
-    pack(zin, zpack)
-    send_cols(zpack, zcol, zhalo_send, zhalo_recv)
-    send_rows(zones, zrow, zcorner, zhalo_send, zhalo_recv)
-
-    inner = pl.ds(1, TILES - 2)
 
     def turned(matrix, slot):
         buffer = turn if matrix.dtype == F32 else iturn
@@ -157,9 +145,13 @@
     def write_ids(r, t, value):
         ids[r, t] = value
 
-    drain(pin.at[inner], load_sem.at[0, 2])
     load_planes(pin, write_prior)
+    drain(zin.at[0], load_sem.at[1, 0])
+    drain(zin.at[TILES - 1], load_sem.at[1, 1])
+    pack(zin, zpack)
     drain(zin.at[inner], load_sem.at[1, 2])
+    send_cols(zpack, zcol, zhalo_send, zhalo_recv)
+    send_rows(zin, zrow, zcorner, zhalo_send, zhalo_recv)
     load_planes(zin, write_ids)
 
     hi_iota = lax.broadcasted_iota(I32, (32, 128), 0)
@@ -265,17 +257,19 @@
 
     start_a(0, scatter(counts))
 
-    def fill_halo(depth, get, put, row_in, col_in, corner_in, sems):
-        def mirrored(j, t, value):
-            return jnp.where(mirror_top, get(j - 1, t), jnp.where(mirror_bottom, get(STEP - j, t), value))
-
-        drain(col_in, sems.at[1])
+    def fill_sides(depth, put, col_in, sem):
+        drain(col_in, sem)
         east = pltpu.roll(col_in[0], 120, 1)
         west = col_in[1]
         for k in range(1, depth + 1):
             both = jnp.where(q < 4, spread(west[8 - k : 9 - k]), spread(east[k - 1 : k]))
             for r in range(STEP):
                 put(r, 15 + k, pltpu.roll(both, (128 - 8 * r) % 128, 1) if r else both)
+
+    def fill_ends(depth, get, put, row_in, corner_in, sems):
+        def mirrored(j, t, value):
+            return jnp.where(mirror_top, get(j - 1, t), jnp.where(mirror_bottom, get(STEP - j, t), value))
+
         drain(corner_in, sems.at[2])
         for k in range(1, depth):
             near, far = jnp.full((8, 128), k - 1, I32), jnp.full((8, 128), 128 - k, I32)
@@ -285,15 +279,12 @@
                 value = jnp.where(s < 4, spread(north[8 - j : 9 - j]), spread(south[j - 1 : j]))
                 put(15 + j, 15 + k, mirrored(j, 15 + k, value))
         drain(row_in, sems.at[0])
-        q_wide = lax.broadcasted_iota(I32, (8, COLS), 0)
         for j in range(1, depth + 1):
-            wide = jnp.where(
-                q_wide < 4,
-                spread(row_in[0, 8 - j : 9 - j, :], (8, COLS)),
-                spread(row_in[1, j - 1 : j, :], (8, COLS)),
-            )
-            rows = jnp.concatenate([wide[:, tile(t)] for t in range(TILES)], axis=0)
-            for t, value in enumerate(turned(rows, j % 4)):
+            rows = []
+            for t in range(TILES):
+                north, south = row_in[0, t, 8 - j : 9 - j, :], row_in[1, t, j - 1 : j, :]
+                rows.append(jnp.where(q < 4, spread(north), spread(south)))
+            for t, value in enumerate(turned(jnp.concatenate(rows, axis=0), j % 4)):
                 put(15 + j, t, mirrored(j, t, value))
 
     def sweeper(src, dst):
@@ -342,8 +333,6 @@
         return span, beyond
 
     def outer_rows(beyond, span, left):
-        for row in range(STEP):
-            beyond(row, left)
         for j in range(1, left + 1):
             span(15 + j, 0, STEP)
             beyond(15 + j, left - j)
@@ -356,15 +345,19 @@
     def put_prior(row, t, value):
         level0[row, t] = value
 
-    fill_halo(DEPTH, lambda row, t: level0[row, t], put_prior, prow, pcol, pcorner, halo_recv)
+    fill_sides(DEPTH, put_prior, pcol, halo_recv.at[1])
     for n in range(1, SWEEPS + 1):
         span, beyond = sweeper(level[n - 1], level[n])
-        for row in range(STEP):
-            if n <= row < STEP - n:
-                span(row, 0, n)
-                span(row, STEP - n, STEP)
-            else:
-                span(row, 0, STEP)
+        for row in range(n, STEP - n):
+            span(row, 0, n)
+            span(row, STEP - n, STEP)
+            beyond(row, DEPTH - n)
+    fill_ends(DEPTH, lambda row, t: level0[row, t], put_prior, prow, pcorner, halo_recv)
+    for n in range(1, SWEEPS + 1):
+        span, beyond = sweeper(level[n - 1], level[n])
+        for row in [*range(n), *range(STEP - n, STEP)]:
+            span(row, 0, STEP)
+            beyond(row, DEPTH - n)
         outer_rows(beyond, span, DEPTH - n)
 
     start_a(1, scatter([block_sums(level3, h) for h in range(2)]))
@@ -373,7 +366,8 @@
     def put_ids(row, t, value):
         ids[row, t] = value
 
-    fill_halo(IDS, lambda row, t: ids[row, t], put_ids, zrow, zcol, zcorner, zhalo_recv)
+    fill_sides(IDS, put_ids, zcol, zhalo_recv.at[1])
+    fill_ends(IDS, lambda row, t: ids[row, t], put_ids, zrow, zcorner, zhalo_recv)
 
     def beside_ids(cells, own_cells):
         other = jnp.full((8, 128), -1, I32)
@@ -431,14 +425,24 @@
         span, beyond = sweeper(level[(n + 2) % 4], level[n - 1] if n < SWEEPS else final)
         for row in range(STEP):
             span(row, 0, STEP)
+            beyond(row, SWEEPS - n)
         outer_rows(beyond, span, SWEEPS - n)
 
     start_a(2, scatter([block_sums(final, h) for h in range(2)]))
+    for r in range(STEP):
+        slot = r % 4
+        values = final[r]
+        values = jnp.where(ids[r, 0:STEP] == own[r // 8], values, -values)
+        for t in range(STEP):
+            turn.at[slot][pl.ds(t, 8, stride=STEP), :] = values[t]
+        rows = turn[slot].T
+        for t in range(TILES):
+            signed.at[t][pl.ds(r, 8, stride=STEP), :] = rows[8 * t : 8 * t + 8]
     start_b(2)
     pairs = factors_of(lookup(share(1, target / finish_b(2)), 5))
-    for r in range(STEP):
-        mine, east = pairs[r // 8]
-        final[r] = final[r] * jnp.where(ids[r, 0:STEP] == own[r // 8], mine, east)
+    for h in range(2):
+        scales[2 * h] = pairs[h][0]
+        scales[2 * h + 1] = -pairs[h][1]
 
     for sems, shapes in ((halo_send, (prow, pcol, pcorner)), (zhalo_send, (zrow, zcol, zcorner))):
         for m, ref in enumerate(shapes):
@@ -450,22 +454,20 @@
         drain(factors.at[n, core], c_send.at[n])
 
 
-def finish(final, out, turn, pout, store_sem):
-    for h in range(2):
-        for r in range(8 * h, 8 * h + 8):
-            slot = r % 4
-            for t in range(STEP):
-                turn.at[slot][pl.ds(t, 8, stride=STEP), :] = final[r, t]
-            rows = turn[slot].T
-            for t in range(TILES):
-                pout.at[t][pl.ds(r, 8, stride=STEP), :] = rows[8 * t : 8 * t + 8]
-        for t in range(TILES):
-            pltpu.make_async_copy(
-                pout.at[t].reshape(8, STEP, 128).at[:, 8 * h : 8 * h + 8, :],
-                out.reshape(8, STEP, COLS).at[:, 8 * h : 8 * h + 8, 128 * t : 128 * t + 128],
-                store_sem,
-            ).start()
-    drain(pout, store_sem)
+def finish(signed, scales, out, lines, result, store_sem):
+    for n in range(4):
+        value = scales[n]
+        cells = [jnp.broadcast_to(value[q : q + 1], (STEP, 128)) for q in range(8)]
+        lines[n] = jnp.concatenate(cells, axis=0).T
+    for t in range(TILES):
+        for b in range(ROWS // 8):
+            row, h = 8 * t + b // 2, b % 2
+            value = signed[t, 8 * b : 8 * b + 8, :]
+            mine = jnp.broadcast_to(lines[2 * h, row : row + 1, :], (8, 128))
+            east = jnp.broadcast_to(lines[2 * h + 1, row : row + 1, :], (8, 128))
+            result[t, 8 * b : 8 * b + 8, :] = value * jnp.where(value > 0, mine, east)
+        pltpu.make_async_copy(result.at[t], out.at[:, 128 * t : 128 * t + 128], store_sem).start()
+    drain(result, store_sem)
 
 
 def body(prior, zone_ids, rate):
@@ -473,11 +475,14 @@
     vmem = pltpu.VMEM
     outside = pl.BlockSpec(memory_space=pltpu.HBM)
     inside = pl.BlockSpec(memory_space=pltpu.VMEM)
-    scaled = pl.pallas_call(
+    parts = pl.pallas_call(
         kernel,
-        out_shape=jax.ShapeDtypeStruct((STEP, STEP, 8, 128), F32),
+        out_shape=(
+            jax.ShapeDtypeStruct((TILES, ROWS, 128), F32),
+            jax.ShapeDtypeStruct((4, 8, 128), F32),
+        ),
         in_specs=[outside] * 3,
-        out_specs=inside,
+        out_specs=(inside, inside),
         scratch_shapes=[
             vmem((TILES, ROWS, 128), F32),
             vmem((TILES, ROWS, 128), I32),
@@ -487,11 +492,12 @@
             vmem((SIDE, SIDE, 8, 128), F32),
             vmem((SIDE, SIDE, 8, 128), F32),
             vmem((SIDE, SIDE, 8, 128), F32),
+            vmem((STEP, STEP, 8, 128), F32),
             vmem((STEP + IDS, STEP + IDS, 8, 128), I32),
-            vmem((2, 8, COLS), F32),
+            vmem((2, TILES, 8, 128), F32),
             vmem((2, 8, 128), F32),
             vmem((4, 8, 128), F32),
-            vmem((2, 8, COLS), I32),
+            vmem((2, TILES, 8, 128), I32),
             vmem((2, 8, 128), I32),
             vmem((4, 8, 128), I32),
             vmem((2, 8, 128), F32),
@@ -524,11 +530,11 @@
     return pl.pallas_call(
         finish,
         out_shape=jax.ShapeDtypeStruct((ROWS, COLS), F32),
-        in_specs=[inside],
+        in_specs=[inside, inside],
         out_specs=outside,
         scratch_shapes=[vmem((4, 128, 128), F32), vmem((TILES, ROWS, 128), F32), dma],
         compiler_params=pltpu.CompilerParams(vmem_limit_bytes=32 * 1024 * 1024),
-    )(scaled)
+    )(*parts)
 
 
 def solution(mesh):

time: 37 us -> 36.7 us (level)
  Pallas kernels: 36.1 us -> 35.7 us
    pallas_call x1, Pallas kernels: 1.48 us -> 1.08 us  [body(): pl.pallas_call(finish, out_shape=jax.ShapeDtypeStruct((ROWS, COLS), F32),...]
where the time goes in v2:
time: 36.7 us; the launch traced here: 36.4 us
  Pallas kernels  35.7 us (97%)
  local copies, waits for them, and re-layouts  0.72 us (2%)
    pallas_call x1, Pallas kernels, body(): pl.pallas_call(kernel, out_shape=(jax.ShapeDtypeStruct((TILES, ROWS, 128)...  34.6 us
    pallas_call x1, Pallas kernels, body(): pl.pallas_call(finish, out_shape=jax.ShapeDtypeStruct((ROWS, COLS), F32),...  1.08 us

profile of v2, /device:TPU:1, one launch (start us, length us, event | category | flops | bytes accessed | tf_op | source)
XLA Modules:
  0.0 36.4 jit_solution(5392330604681683180)
XLA Ops:
  0.0 0.0 copy-start
  0.0 0.7 %copy-done = f32[4096]{0:T(1024)S(1)} copy-done((f32[4096]{0:T(1024)S(1)}, f32[4096]{0:T(1024)}, u32[]{:S(2)}) %copy-start) | copy-done | bytes 16408
  0.7 34.6 %shard_map.37 = (f32[16,128,128]{2,1,0:T(8,128)S(1)}, f32[4,8,128]{2,1,0:T(8,128)S(1)}) custom-call(f32[128,2048]{1,0:T(8,128)} %prior.1, s32[128,2048]{1,0:T(8,128)} %zones.1, f32[2,16,128]{2,1,0:T(8,128)S(1)} %bitcast.1), custom_call_target="tpu_custom_call" | custom-call | tf_op jit(solution)/shard_map/pallas_call | solution.py:478
  35.4 1.1 %shard_map.38 = f32[128,2048]{1,0:T(8,128)} custom-call(f32[16,128,128]{2,1,0:T(8,128)S(1)} %get-tuple-element.7.signed, f32[4,8,128]{2,1,0:T(8,128)S(1)} %get-tuple-element.8.scales), custom_call_target="tpu_custom_call" | custom-call | tf_op jit(solution)/shard_map/pallas_call | solution.py:530
Async XLA Ops:
  0.0 0.7 %copy-start = (f32[4096]{0:T(1024)S(1)}, f32[4096]{0:T(1024)}, u32[]{:S(2)}) copy-start(f32[4096]{0:T(1024)} %param.5) | copy-start | bytes 49156

commit v3 on v2

--- a/solution.py
+++ b/solution.py
@@ -108,9 +108,9 @@
             device_id=place(lat + dr, lon + dc), device_id_type=MESH,
         ).start()
 
-    def send_rows(source, row_in, corner_in, out_sem, in_sem):
-        send(source.at[:, first8, :], row_in.at[1], out_sem.at[0], in_sem.at[0], -1, 0)
-        send(source.at[:, last8, :], row_in.at[0], out_sem.at[0], in_sem.at[0], 1, 0)
+    def send_rows(source, row_in, corner_in, out_sem, in_sem, depth):
+        send(source.at[:, pl.ds(0, depth), :], row_in.at[1, :, pl.ds(0, depth), :], out_sem.at[0], in_sem.at[0], -1, 0)
+        send(source.at[:, pl.ds(ROWS - depth, depth), :], row_in.at[0, :, pl.ds(8 - depth, depth), :], out_sem.at[0], in_sem.at[0], 1, 0)
         send(source.at[0, first8, :], corner_in.at[2], out_sem.at[2], in_sem.at[2], -1, -1)
         send(source.at[TILES - 1, first8, :], corner_in.at[3], out_sem.at[2], in_sem.at[2], -1, 1)
         send(source.at[0, last8, :], corner_in.at[0], out_sem.at[2], in_sem.at[2], 1, -1)
@@ -125,8 +125,8 @@
     pack(pin, ppack)
     drain(pin.at[inner], load_sem.at[0, 2])
     pl.semaphore_wait(barrier, greeted)
-    send_rows(pin, prow, pcorner, halo_send, halo_recv)
     send_cols(ppack, pcol, halo_send, halo_recv)
+    send_rows(pin, prow, pcorner, halo_send, halo_recv, DEPTH)
 
     def turned(matrix, slot):
         buffer = turn if matrix.dtype == F32 else iturn
@@ -151,7 +151,7 @@
     pack(zin, zpack)
     drain(zin.at[inner], load_sem.at[1, 2])
     send_cols(zpack, zcol, zhalo_send, zhalo_recv)
-    send_rows(zin, zrow, zcorner, zhalo_send, zhalo_recv)
+    send_rows(zin, zrow, zcorner, zhalo_send, zhalo_recv, IDS)
     load_planes(zin, write_ids)
 
     hi_iota = lax.broadcasted_iota(I32, (32, 128), 0)
@@ -278,7 +278,7 @@
             for j in range(1, depth + 1 - k):
                 value = jnp.where(s < 4, spread(north[8 - j : 9 - j]), spread(south[j - 1 : j]))
                 put(15 + j, 15 + k, mirrored(j, 15 + k, value))
-        drain(row_in, sems.at[0])
+        drain(row_in.at[:, :, pl.ds(0, depth), :], sems.at[0])
         for j in range(1, depth + 1):
             rows = []
             for t in range(TILES):
@@ -444,7 +444,9 @@
         scales[2 * h] = pairs[h][0]
         scales[2 * h + 1] = -pairs[h][1]
 
-    for sems, shapes in ((halo_send, (prow, pcol, pcorner)), (zhalo_send, (zrow, zcol, zcorner))):
+    shapes0 = (prow.at[:, :, pl.ds(0, DEPTH), :], pcol, pcorner)
+    shapes1 = (zrow.at[:, :, pl.ds(0, IDS), :], zcol, zcorner)
+    for sems, shapes in ((halo_send, shapes0), (zhalo_send, shapes1)):
         for m, ref in enumerate(shapes):
             drain(ref, sems.at[m])
     for n in range(3):

time: 36.7 us -> 36.5 us (level)
  no operation moved by 1% of the time
where the time goes in v3:
time: 36.5 us; the launch traced here: 36.3 us
  Pallas kernels  35.5 us (97%)
  local copies, waits for them, and re-layouts  0.72 us (2%)
    pallas_call x1, Pallas kernels, body(): pl.pallas_call(kernel, out_shape=(jax.ShapeDtypeStruct((TILES, ROWS, 128)...  34.5 us
    pallas_call x1, Pallas kernels, body(): pl.pallas_call(finish, out_shape=jax.ShapeDtypeStruct((ROWS, COLS), F32),...  1.08 us

profile of v3, /device:TPU:1, one launch (start us, length us, event | category | flops | bytes accessed | tf_op | source)
XLA Modules:
  0.0 36.3 jit_solution(1478340643795100375)
XLA Ops:
  0.0 0.0 copy-start
  0.0 0.7 %copy-done = f32[4096]{0:T(1024)S(1)} copy-done((f32[4096]{0:T(1024)S(1)}, f32[4096]{0:T(1024)}, u32[]{:S(2)}) %copy-start) | copy-done | bytes 16408
  0.7 34.5 %shard_map.37 = (f32[16,128,128]{2,1,0:T(8,128)S(1)}, f32[4,8,128]{2,1,0:T(8,128)S(1)}) custom-call(f32[128,2048]{1,0:T(8,128)} %prior.1, s32[128,2048]{1,0:T(8,128)} %zones.1, f32[2,16,128]{2,1,0:T(8,128)S(1)} %bitcast.1), custom_call_target="tpu_custom_call" | custom-call | tf_op jit(solution)/shard_map/pallas_call | solution.py:480
  35.2 1.1 %shard_map.38 = f32[128,2048]{1,0:T(8,128)} custom-call(f32[16,128,128]{2,1,0:T(8,128)S(1)} %get-tuple-element.7.signed, f32[4,8,128]{2,1,0:T(8,128)S(1)} %get-tuple-element.8.scales), custom_call_target="tpu_custom_call" | custom-call | tf_op jit(solution)/shard_map/pallas_call | solution.py:532
Async XLA Ops:
  0.0 0.7 %copy-start = (f32[4096]{0:T(1024)S(1)}, f32[4096]{0:T(1024)}, u32[]{:S(2)}) copy-start(f32[4096]{0:T(1024)} %param.5) | copy-start | bytes 49156
